TPU v7x, 128 devices: a whole 4x4x4 slice. The times are simulated.
128 devices in a mesh: tm: 16 (over x, z_hi, core), freq: 8 (over y, z_lo).
Axes of the slice: x: 4, y: 4, z: 4 (z_hi: 2, z_lo: 2; z = z_hi * 2 + z_lo), core: 2. Of those that a mesh axis runs over, the one named last changes fastest.
Arguments:
- visibility: bfloat16 [2, 32, 1024, 4096], P(None, None, 'freq', 'tm'), may hold values from -6 to 6
- spectrum_power_sum: float32 [1024, 4096], P('freq', 'tm'), may hold values from 50 to 500, as said below
- square_sum: float32 [1024, 4096], P('freq', 'tm'), as said below
- accum_count: int32 [1024, 4096], P('freq', 'tm'), may hold values from 64 to 256
- rfi_mask: int32 [1024, 4096], P('freq', 'tm'), may hold values 0 or 1
- baseline_delay_class: int32 [32, 1], P('freq'), may hold values from 0 to 3
- filter_bank: bfloat16 [4, 1024, 1024], replicated, may hold values from -0.1875 to 0.1875
Outputs:
- filtered: bfloat16 [2, 32, 1024, 4096], P(None, 'freq', None, 'tm')
Inputs may be any that keep to these rules, and one draw needn't show every extreme that they name: `spectrum_power_sum`: positive in every sample. `square_sum`: positive in every sample.
All inputs are finite; a program needn't handle non-finite values. No bound on the sum of `rfi_mask` on one device may be relied on, other than what follows from the above.
Results may differ from a plain program's by a relative error of at most 0.0043.
The roundings to bfloat16 on the way count: a program that leaves them out, or rounds other values in their place, can miss the bound.
Values may be sent and summed in bfloat16 or wider, within the bound.
A program may use at most 128 MiB of HBM per device.

v0:
```python
import math
import jax
import jax.numpy as jnp
from jax import lax
from jax.sharding import PartitionSpec as P

RIM = 16


def padded_2(value, sides, width):
    for axis, dim in sides:
        devices, length = (lax.axis_size(axis), value.shape[dim])
        up = [(i, (i + 1) % devices) for i in range(devices)]
        down = [(j, i) for i, j in up]
        last = lax.slice_in_dim(value, length - width, length, axis=dim)
        leading = lax.slice_in_dim(value, 0, width, axis=dim)
        before = lax.ppermute(last, axis, up)
        after = lax.ppermute(leading, axis, down)
        value = jnp.concatenate([before, value, after], axis=dim)
    return value


def rotation_table(rows_n, cols_n, period):
    row_index = jnp.arange(rows_n, dtype=jnp.int32)
    col_index = jnp.arange(cols_n, dtype=jnp.int32)
    phase = row_index[:, None] * col_index[None, :] % period
    angles = 2.0 * math.pi / period * phase.astype(jnp.float32)
    cosine = jnp.cos(angles)
    sine = jnp.sin(angles)
    real_row = jnp.stack([cosine, sine])
    imag_row = jnp.stack([-sine, cosine])
    return jnp.stack([real_row, imag_row])


def twist_table(rows_n, cols_n, period):
    row_index = jnp.arange(rows_n, dtype=jnp.int32)
    col_index = jnp.arange(cols_n, dtype=jnp.int32)
    phase = row_index[:, None] * col_index[None, :] % period
    angles = 2.0 * math.pi / period * phase.astype(jnp.float32)
    return (jnp.cos(angles), jnp.sin(angles))


def sidereal_transform(received):
    periods = lax.axis_size("tm")
    samples = received.shape[3]
    inner_len = samples // periods
    base_n = received.shape[1]
    chan_n = received.shape[2]
    widened = received.astype(jnp.float32).reshape(2, base_n, chan_n, periods, inner_len)
    better = lax.Precision.HIGH
    first_table = rotation_table(periods, periods, periods)
    stepped = jnp.einsum("cbfps,dcjp->dbfjs", widened, first_table, precision=better)
    cos_two, sin_two = twist_table(periods, inner_len, samples)
    twist_real = stepped[0] * cos_two + stepped[1] * sin_two
    twist_imag = stepped[1] * cos_two - stepped[0] * sin_two
    twisted = jnp.stack([twist_real, twist_imag])
    tertiary_lookup = rotation_table(inner_len, inner_len, inner_len)
    finished = jnp.einsum("cbfjs,dcks->dbfkj", twisted, tertiary_lookup, precision=better)
    norm_scale = 1.0 / math.sqrt(samples)
    finished = finished.reshape(2, base_n, chan_n, samples) * norm_scale
    return finished.astype(jnp.bfloat16)


def shards(
    visibility,
    spectrum_power_sum,
    square_sum,
    accum_count,
    rfi_mask,
    baseline_delay_class,
    filter_bank,
):
    counts = accum_count.astype(jnp.float32)
    kurtosis = (
        (counts + 1.0)
        / (counts - 1.0)
        * (counts * square_sum / (spectrum_power_sum * spectrum_power_sum) - 1.0)
    )
    flag_weight = rfi_mask.astype(jnp.float32) * jnp.exp(-2.0 * (kurtosis - 1.0) ** 2)
    local_len = flag_weight.shape[1]
    padded = padded_2(flag_weight, (("tm", 1),), RIM)
    smooth_weight = jnp.zeros(flag_weight.shape, jnp.float32)
    for offset in range(2 * RIM + 1):
        factor = (RIM + 1 - abs(offset - RIM)) / float((RIM + 1) ** 2)
        smooth_weight = smooth_weight + factor * padded[:, offset : offset + local_len]
    weighted = (visibility.astype(jnp.float32) * smooth_weight[None, None]).astype(jnp.bfloat16)
    spectrum = sidereal_transform(
        lax.all_to_all(weighted, "tm", split_axis=2, concat_axis=3, tiled=True)
    )
    chosen = jnp.take(filter_bank, baseline_delay_class[:, 0], axis=0)
    moved = lax.all_to_all(spectrum, "tm", split_axis=3, concat_axis=2, tiled=True)
    return jnp.einsum(
        "bgf,cbfm->cbgm",
        chosen,
        lax.all_to_all(moved, "freq", split_axis=1, concat_axis=2, tiled=True),
        preferred_element_type=jnp.float32,
    ).astype(jnp.bfloat16)


def solution(mesh):
    in_specs = (
        P(None, None, "freq", "tm"),
        P("freq", "tm"),
        P("freq", "tm"),
        P("freq", "tm"),
        P("freq", "tm"),
        P("freq", None),
        P(),
    )
    out_specs = P(None, "freq", None, "tm")
    return jax.shard_map(shards, mesh=mesh, in_specs=in_specs, out_specs=out_specs, check_vma=False)
```

profile of v0, /device:TPU:0, one launch (start us, length us, event | category | flops | bytes accessed | tf_op | source)
XLA Modules:
  0.0 342.9 jit_solution(15936010906509529654)
XLA Ops:
  0.0 1.2 exponential_multiply_fusion
  1.2 0.1 fusion.152
  1.3 5.7 %collective-permute-start.1 = (f32[128,16]{1,0:T(8,128)S(1)}, f32[128,16]{1,0:T(8,128)S(1)}, u32[]{:S(2)}, u32[]{:S(2)}) collective-permute-start(f32[128,16]{1,0:T(8,128)S(1)} %get-tuple-element.12), channel_id=1, source_target_pairs={{8,0},{16,8},{24,16},{32,24},{40,32},{48,40},{56,48},{64,56},{72,6... | collective-permute-start | bytes 24584 | tf_op jit(solution)/shard_map/ppermute | solution.py:18
  7.0 1.9 collective-permute-done
  8.9 1.7 fusion.33
  10.6 7.2 %multiply_convert_fusion = bf16[2,32,128,256]{3,1,0,2:T(8,128)(2,1)} fusion(bf16[2,32,128,256]{3,2,1,0:T(8,128)(2,1)} %param.7, f32[128,256]{1,0:T(8,128)S(1)} %fusion.33), kind=kLoop, calls=%fused_computation.13 | loop fusion | flops 6291456 | bytes 8519680 | tf_op jit(solution)/shard_map/convert_element_type | solution.py:86
  17.7 6.8 %all-to-all-start = ((bf16[2,32,128,256]{3,1,0,2:T(8,128)(2,1)}), bf16[2,32,128,256]{3,1,0,2:T(8,128)(2,1)}, u32[]{:S(2)}, u32[]{:S(2)}) async-start(bf16[2,32,128,256]{3,1,0,2:T(8,128)(2,1)} %multiply_convert_fusion), calls=%async_computation | async-start | bytes 8388608 | tf_op jit(solution)/shard_map/all_to_all | solution.py:88
  24.6 0.1 fusion.145
  24.6 0.1 fusion.143
  24.7 0.1 fusion.138
  24.8 1.0 fusion.126
  25.8 1.0 fusion.124
  26.8 0.1 maximum_bitcast_fusion.2
  26.9 50.1 %all-to-all-done = bf16[2,32,128,256]{3,1,0,2:T(8,128)(2,1)} async-done(((bf16[2,32,128,256]{3,1,0,2:T(8,128)(2,1)}), bf16[2,32,128,256]{3,1,0,2:T(8,128)(2,1)}, u32[]{:S(2)}, u32[]{:S(2)}) %all-to-all-start) | async-done | bytes 4194336 | tf_op jit(solution)/shard_map/all_to_all | solution.py:88
  77.0 9.8 %fusion.15 = f32[2,32,8,16,256]{4,3,2,1,0:T(8,128)S(1)} fusion(bf16[2,32,16,8,256]{4,1,0,3,2:T(8,128)(2,1)} %bitcast.8, f32[1,2,16,16]{3,2,1,0:T(8,128)S(1)} %get-tuple-element.14, f32[1,2,16,16]{3,2,1,0:T(8,128)S(1)} %get-tuple-element.13), kind=kOutput, calls=%fused_computation.23 | convolution fusion | flops 402654208 | bytes 12587008 | tf_op jit(solution)/shard_map/cbfps,dcjp->dbfjs/dot_general | solution.py:52
  86.8 1.9 multiply_add_fusion
  88.7 1.8 pad_maximum_fusion
  90.5 11.1 %fusion.10 = bf16[2,32,8,256,16]{3,1,4,2,0:T(8,128)(2,1)} fusion(f32[2,32,8,16,256]{4,3,2,1,0:T(8,128)S(1)} %pad_maximum_fusion, f32[1,2,256,256]{3,2,1,0:T(8,128)S(1)} %get-tuple-element.10, f32[1,2,256,256]{3,2,1,0:T(8,128)S(1)} %get-tuple-element.9), kind=kOutput, calls=%fused_computation.15 | convolution fusion | flops 6446907392 | bytes 13631488 | tf_op jit(solution)/shard_map/cbfjs,dcks->dbfkj/dot_general | solution.py:58
  101.6 23.2 %copy.33 = bf16[2,32,8,256,16]{1,2,0,4,3:T(8,128)(2,1)} copy(bf16[2,32,8,256,16]{3,1,4,2,0:T(8,128)(2,1)} %fusion.10) | data formatting | bytes 8388608 | tf_op jit(solution)/shard_map/convert_element_type | solution.py:61
  124.8 20.7 %reshape.226 = bf16[16,2,65536]{2,1,0:T(2,128)(2,1)} reshape(bf16[4096,2,8,32]{3,2,1,0:T(8,128)(2,1)} %bitcast.74) | data formatting | bytes 8388608
  145.5 65.0 %all_to_all.51 = bf16[16,2,65536]{2,1,0:T(2,128)(2,1)} all-to-all(bf16[16,2,65536]{2,1,0:T(2,128)(2,1)} %reshape.226), channel_id=1, replica_groups=mesh['tm'=16,'freq'=8] {'tm'}, dimensions={0} | all-to-all | bytes 8388608 | tf_op jit(solution)/shard_map/all_to_all | solution.py:91
  210.5 16.0 %reshape.227 = bf16[4096,2,8,32]{3,2,1,0:T(8,128)(2,1)} reshape(bf16[16,2,65536]{2,1,0:T(2,128)(2,1)} %all_to_all.51) | data formatting | bytes 8388608
  226.5 19.5 %copy.22 = bf16[2,32,16,8,256]{4,3,2,0,1:T(8,128)(2,1)} copy(bf16[2,32,16,8,256]{1,3,0,4,2:T(8,128)(2,1)} %bitcast.75) | data formatting | bytes 8388608 | tf_op jit(solution)/shard_map/all_to_all | solution.py:91
  246.0 5.7 %all-to-all-start.2 = ((bf16[2,32,128,256]{3,2,0,1:T(8,128)(2,1)}), bf16[2,32,128,256]{3,2,0,1:T(8,128)(2,1)}, u32[]{:S(2)}, u32[]{:S(2)}) async-start(bf16[2,32,128,256]{3,2,0,1:T(8,128)(2,1)} %bitcast.76), calls=%async_computation.2 | async-start | bytes 8388608 | tf_op jit(solution)/shard_map/all_to_all | solution.py:95
  251.8 5.9 %fusion.151 = (bf16[4,512,1024]{2,1,0:T(8,128)(2,1)}, bf16[4,512,1024]{2,1,0:T(8,128)(2,1)}) fusion(bf16[4,1024,1024]{2,1,0:T(8,128)(2,1)} %param.13), kind=kLoop, calls=%fused_computation.234 | loop fusion | bytes 16777216 | tf_op jit(solution)/shard_map/jit(_take)/gather | solution.py:90
  257.6 5.0 %gather_fusion = bf16[4,512,1024]{2,1,0:T(8,128)(2,1)} fusion(bf16[4,512,1024]{2,1,0:T(8,128)(2,1)} %get-tuple-element.7, s32[1024]{0:T(1024)S(1)} %pad_clamp_fusion), kind=kCustom, calls=%fused_computation | custom fusion | bytes 8388624 | tf_op jit(solution)/shard_map/jit(_take)/gather | solution.py:90
  262.6 5.0 %gather_fusion.1 = bf16[4,512,1024]{2,1,0:T(8,128)(2,1)} fusion(bf16[4,512,1024]{2,1,0:T(8,128)(2,1)} %get-tuple-element.8, s32[1024]{0:T(1024)S(1)} %pad_clamp_fusion), kind=kCustom, calls=%fused_computation.1 | custom fusion | bytes 8388624 | tf_op jit(solution)/shard_map/jit(_take)/gather | solution.py:90
  267.6 43.1 %all-to-all-done.2 = bf16[2,32,128,256]{3,2,0,1:T(8,128)(2,1)} async-done(((bf16[2,32,128,256]{3,2,0,1:T(8,128)(2,1)}), bf16[2,32,128,256]{3,2,0,1:T(8,128)(2,1)}, u32[]{:S(2)}, u32[]{:S(2)}) %all-to-all-start.2) | async-done | bytes 4194336 | tf_op jit(solution)/shard_map/all_to_all | solution.py:95
  310.7 7.5 %copy.24 = bf16[2,4,8,128,256]{3,2,4,0,1:T(8,128)(2,1)} copy(bf16[2,4,8,128,256]{4,3,0,1,2:T(8,128)(2,1)} %bitcast.26) | data formatting | bytes 8388608 | tf_op jit(solution)/shard_map/all_to_all | solution.py:95
  318.2 7.3 %all_to_all.47 = bf16[2,4,1024,256]{2,3,0,1:T(8,128)(2,1)} reshape(bf16[2,4,8,128,256]{3,2,4,0,1:T(8,128)(2,1)} %copy.24) | data formatting | bytes 8388608 | tf_op jit(solution)/shard_map/all_to_all | solution.py:95
  325.5 11.2 %convert_bitcast_fusion = bf16[2,4,1024,256]{2,3,0,1:T(8,128)(2,1)} fusion(bf16[2,4,1024,256]{2,3,0,1:T(8,128)(2,1)} %all_to_all.47, bf16[4,512,1024]{2,1,0:T(8,128)(2,1)} %gather_fusion.1, bf16[4,512,1024]{2,1,0:T(8,128)(2,1)} %gather_fusion, pred[4]{0:T(512)(128)(4,1)S(1)} %and_bitcast_fusion), kind=kOutput, calls=%fused_computation.19 | convolution fusion | flops 4318035968 | bytes 16777220 | tf_op jit(solution)/shard_map/bgf,cbfm->cbgm/dot_general | solution.py:92
  336.7 6.2 %copy.25 = bf16[2,4,1024,256]{3,2,1,0:T(8,128)(2,1)} copy(bf16[2,4,1024,256]{2,3,0,1:T(8,128)(2,1)} %convert_bitcast_fusion) | data formatting | bytes 8388608 | tf_op jit(solution)/shard_map/convert_element_type | solution.py:97
  (8 shorter events, 0.1 us)
Async XLA Ops:
  1.3 7.6 %collective-permute-start = (f32[128,16]{1,0:T(8,128)S(1)}, f32[128,16]{1,0:T(8,128)S(1)}, u32[]{:S(2)}, u32[]{:S(2)}) collective-permute-start(f32[128,16]{1,0:T(8,128)S(1)} %get-tuple-element.11), channel_id=1, source_target_pairs={{0,8},{8,16},{16,24},{24,32},{32,40},{40,48},{48,56},{56,64},{64,7... | collective-permute-start | bytes 24584 | tf_op jit(solution)/shard_map/ppermute | solution.py:17
  1.3 7.6 %collective-permute-start.1 = (f32[128,16]{1,0:T(8,128)S(1)}, f32[128,16]{1,0:T(8,128)S(1)}, u32[]{:S(2)}, u32[]{:S(2)}) collective-permute-start(f32[128,16]{1,0:T(8,128)S(1)} %get-tuple-element.12), channel_id=1, source_target_pairs={{8,0},{16,8},{24,16},{32,24},{40,32},{48,40},{56,48},{64,56},{72,6... | collective-permute-start | bytes 24584 | tf_op jit(solution)/shard_map/ppermute | solution.py:18
  17.7 59.3 %all-to-all-start = ((bf16[2,32,128,256]{3,1,0,2:T(8,128)(2,1)}), bf16[2,32,128,256]{3,1,0,2:T(8,128)(2,1)}, u32[]{:S(2)}, u32[]{:S(2)}) async-start(bf16[2,32,128,256]{3,1,0,2:T(8,128)(2,1)} %multiply_convert_fusion), calls=%async_computation | async-start | bytes 8388608 | tf_op jit(solution)/shard_map/all_to_all | solution.py:88
  246.0 5.7 %copy-start = (s32[4,1]{0,1:T(1,128)S(1)}, s32[4,1]{0,1:T(1,128)}, u32[]{:S(2)}) copy-start(s32[4,1]{0,1:T(1,128)} %param.12) | copy-start | bytes 52
  246.0 64.7 %all-to-all-start.2 = ((bf16[2,32,128,256]{3,2,0,1:T(8,128)(2,1)}), bf16[2,32,128,256]{3,2,0,1:T(8,128)(2,1)}, u32[]{:S(2)}, u32[]{:S(2)}) async-start(bf16[2,32,128,256]{3,2,0,1:T(8,128)(2,1)} %bitcast.76), calls=%async_computation.2 | async-start | bytes 8388608 | tf_op jit(solution)/shard_map/all_to_all | solution.py:95
where the time goes:
time: 345 us; the launch traced here: 343 us
  local copies, waits for them, and re-layouts  116 us (34%)
  waiting for transfers between devices  95.1 us (28%)
  blocking collectives  65 us (19%)
  matrix products  32.1 us (9%)
  starting transfers between devices  18.3 us (5%)
  other arithmetic  16 us (5%)
    all_to_all x1, blocking collectives, shards(): lax.all_to_all(spectrum, 'tm', split_axis=3, concat_axis=2, tiled=True)  65 us
    all_to_all x1, waiting for transfers between devices, shards(): lax.all_to_all(weighted, 'tm', split_axis=2, concat_axis=3, tiled=True)  50.1 us
    all_to_all x1, waiting for transfers between devices, shards(): lax.all_to_all(moved, 'freq', split_axis=1, concat_axis=2, tiled=True)  43.1 us
    unnamed x4, local copies, waits for them, and re-layouts  36.8 us
    convert_element_type x1, local copies, waits for them, and re-layouts, sidereal_transform(): return finished.astype(jnp.bfloat16)  23.2 us
    all_to_all x1, local copies, waits for them, and re-layouts, shards(): lax.all_to_all(spectrum, 'tm', split_axis=3, concat_axis=2, tiled=True)  19.5 us
    gather x3, local copies, waits for them, and re-layouts, shards(): chosen = jnp.take(filter_bank, baseline_delay_class[:, 0], axis=0)  15.8 us
    all_to_all x2, local copies, waits for them, and re-layouts, shards(): lax.all_to_all(moved, 'freq', split_axis=1, concat_axis=2, tiled=True)  14.8 us
  transfers between devices with their start and end apart: 4, of which 3 were waited for; matrix products, arithmetic and copies ran while one was open for 5% of the time, Pallas kernels for 0%

commit v1 on v0

--- a/solution.py
+++ b/solution.py
@@ -3,8 +3,18 @@
 import jax.numpy as jnp
 from jax import lax
 from jax.sharding import PartitionSpec as P
+from jax.lax import all_to_all, axis_size
 
 RIM = 16
+build_the_digits = lambda inner_x, axis_id, k_dim, out_dim: jnp.concatenate(
+    all_to_all(
+        jnp.stack(jnp.split(inner_x, axis_size(axis_id), axis=k_dim)),
+        axis_name=axis_id,
+        split_axis=0,
+        concat_axis=0,
+    ),
+    out_dim,
+)
 
 
 def padded_2(value, sides, width):
@@ -92,7 +102,7 @@
     return jnp.einsum(
         "bgf,cbfm->cbgm",
         chosen,
-        lax.all_to_all(moved, "freq", split_axis=1, concat_axis=2, tiled=True),
+        build_the_digits(moved, "freq", 1, 2),
         preferred_element_type=jnp.float32,
     ).astype(jnp.bfloat16)
 

time: 345 us -> 356 us (1.032)
  local copies, waits for them, and re-layouts: 116 us -> 128 us
    all_to_all x2 -> x0, local copies, waits for them, and re-layouts: 14.8 us -> none  [shards(): lax.all_to_all(moved, 'freq', split_axis=1, concat_axis=2, tiled=True)]
    reshape x0 -> x2, local copies, waits for them, and re-layouts: none -> 14.8 us  [jnp.concatenate(all_to_all(jnp.stack(jnp.split(inner_x, axis_size(axis_id...]
    unnamed x4 -> x13, local copies, waits for them, and re-layouts: 36.8 us -> 47 us
where the time goes in v1:
time: 356 us; the launch traced here: 354 us
  local copies, waits for them, and re-layouts  128 us (36%)
  waiting for transfers between devices  95 us (27%)
  blocking collectives  65 us (18%)
  matrix products  32.1 us (9%)
  starting transfers between devices  18.3 us (5%)
  other arithmetic  16 us (4%)
    all_to_all x1, blocking collectives, shards(): lax.all_to_all(spectrum, 'tm', split_axis=3, concat_axis=2, tiled=True)  65 us
    all_to_all x1, waiting for transfers between devices, shards(): lax.all_to_all(weighted, 'tm', split_axis=2, concat_axis=3, tiled=True)  50.1 us
    unnamed x13, local copies, waits for them, and re-layouts  47 us
    all_to_all x1, waiting for transfers between devices, all_to_all(jnp.stack(jnp.split(inner_x, axis_size(axis_id), axis=k_dim)),...  43 us
    convert_element_type x1, local copies, waits for them, and re-layouts, sidereal_transform(): return finished.astype(jnp.bfloat16)  23.2 us
    all_to_all x1, local copies, waits for them, and re-layouts, shards(): lax.all_to_all(spectrum, 'tm', split_axis=3, concat_axis=2, tiled=True)  19.5 us
    gather x3, local copies, waits for them, and re-layouts, shards(): chosen = jnp.take(filter_bank, baseline_delay_class[:, 0], axis=0)  15.9 us
    reshape x2, local copies, waits for them, and re-layouts, jnp.concatenate(all_to_all(jnp.stack(jnp.split(inner_x, axis_size(axis_id...  14.8 us
  transfers between devices with their start and end apart: 4, of which 3 were waited for; matrix products, arithmetic and copies ran while one was open for 5% of the time, Pallas kernels for 0%

profile of v1, /device:TPU:0, one launch (start us, length us, event | category | flops | bytes accessed | tf_op | source)
XLA Modules:
  0.0 354.0 jit_solution(11935213101935556060)
XLA Ops:
  0.0 1.2 exponential_multiply_fusion
  1.3 5.7 %collective-permute-start.1 = (f32[128,16]{1,0:T(8,128)S(1)}, f32[128,16]{1,0:T(8,128)S(1)}, u32[]{:S(2)}, u32[]{:S(2)}) collective-permute-start(f32[128,16]{1,0:T(8,128)S(1)} %get-tuple-element.12), channel_id=1, source_target_pairs={{8,0},{16,8},{24,16},{32,24},{40,32},{48,40},{56,48},{64,56},{72,6... | collective-permute-start | bytes 24584 | tf_op jit(solution)/shard_map/ppermute | solution.py:28
  7.0 1.9 collective-permute-done
  8.9 1.7 fusion.41
  10.6 7.2 %multiply_convert_fusion = bf16[2,32,128,256]{3,1,0,2:T(8,128)(2,1)} fusion(bf16[2,32,128,256]{3,2,1,0:T(8,128)(2,1)} %param.7, f32[128,256]{1,0:T(8,128)S(1)} %fusion.41), kind=kLoop, calls=%fused_computation.13 | loop fusion | flops 6291456 | bytes 8519680 | tf_op jit(solution)/shard_map/convert_element_type | solution.py:96
  17.7 6.8 %all-to-all-start = ((bf16[2,32,128,256]{3,1,0,2:T(8,128)(2,1)}), bf16[2,32,128,256]{3,1,0,2:T(8,128)(2,1)}, u32[]{:S(2)}, u32[]{:S(2)}) async-start(bf16[2,32,128,256]{3,1,0,2:T(8,128)(2,1)} %multiply_convert_fusion), calls=%async_computation | async-start | bytes 8388608 | tf_op jit(solution)/shard_map/all_to_all | solution.py:98
  24.8 1.0 fusion.134
  25.8 1.0 fusion.132
  26.9 50.1 %all-to-all-done = bf16[2,32,128,256]{3,1,0,2:T(8,128)(2,1)} async-done(((bf16[2,32,128,256]{3,1,0,2:T(8,128)(2,1)}), bf16[2,32,128,256]{3,1,0,2:T(8,128)(2,1)}, u32[]{:S(2)}, u32[]{:S(2)}) %all-to-all-start) | async-done | bytes 4194336 | tf_op jit(solution)/shard_map/all_to_all | solution.py:98
  77.0 9.8 %fusion.15 = f32[2,32,8,16,256]{4,3,2,1,0:T(8,128)S(1)} fusion(bf16[2,32,16,8,256]{4,1,0,3,2:T(8,128)(2,1)} %bitcast.8, f32[1,2,16,16]{3,2,1,0:T(8,128)S(1)} %get-tuple-element.14, f32[1,2,16,16]{3,2,1,0:T(8,128)S(1)} %get-tuple-element.13), kind=kOutput, calls=%fused_computation.23 | convolution fusion | flops 402654208 | bytes 12587008 | tf_op jit(solution)/shard_map/cbfps,dcjp->dbfjs/dot_general | solution.py:62
  86.8 1.9 multiply_add_fusion
  88.7 1.8 pad_maximum_fusion
  90.5 11.1 %fusion.10 = bf16[2,32,8,256,16]{3,1,4,2,0:T(8,128)(2,1)} fusion(f32[2,32,8,16,256]{4,3,2,1,0:T(8,128)S(1)} %pad_maximum_fusion, f32[1,2,256,256]{3,2,1,0:T(8,128)S(1)} %get-tuple-element.10, f32[1,2,256,256]{3,2,1,0:T(8,128)S(1)} %get-tuple-element.9), kind=kOutput, calls=%fused_computation.15 | convolution fusion | flops 6446907392 | bytes 13631488 | tf_op jit(solution)/shard_map/cbfjs,dcks->dbfkj/dot_general | solution.py:68
  101.6 23.2 %copy.41 = bf16[2,32,8,256,16]{1,2,0,4,3:T(8,128)(2,1)} copy(bf16[2,32,8,256,16]{3,1,4,2,0:T(8,128)(2,1)} %fusion.10) | data formatting | bytes 8388608 | tf_op jit(solution)/shard_map/convert_element_type | solution.py:71
  124.8 20.7 %reshape.234 = bf16[16,2,65536]{2,1,0:T(2,128)(2,1)} reshape(bf16[4096,2,8,32]{3,2,1,0:T(8,128)(2,1)} %bitcast.105) | data formatting | bytes 8388608
  145.5 65.0 %all_to_all.38 = bf16[16,2,65536]{2,1,0:T(2,128)(2,1)} all-to-all(bf16[16,2,65536]{2,1,0:T(2,128)(2,1)} %reshape.234), channel_id=1, replica_groups=mesh['tm'=16,'freq'=8] {'tm'}, dimensions={0} | all-to-all | bytes 8388608 | tf_op jit(solution)/shard_map/all_to_all | solution.py:101
  210.5 16.1 %reshape.235 = bf16[4096,2,8,32]{3,2,1,0:T(8,128)(2,1)} reshape(bf16[16,2,65536]{2,1,0:T(2,128)(2,1)} %all_to_all.38) | data formatting | bytes 8388608
  226.6 19.5 %copy.31 = bf16[2,32,16,8,256]{4,3,2,1,0:T(8,128)(2,1)} copy(bf16[2,32,16,8,256]{1,3,0,4,2:T(8,128)(2,1)} %bitcast.106) | data formatting | bytes 8388608 | tf_op jit(solution)/shard_map/all_to_all | solution.py:101
  246.0 2.0 fusion.31
  248.1 1.9 fusion.30
  249.9 1.9 fusion.29
  251.8 1.9 fusion.28
  254.6 0.8 fusion.26
  257.1 5.7 %all-to-all-start.2 = ((bf16[8,2,4,128,256]{4,3,2,1,0:T(8,128)(2,1)}), bf16[8,2,4,128,256]{4,3,2,1,0:T(8,128)(2,1)}, u32[]{:S(2)}, u32[]{:S(2)}) async-start(bf16[8,2,4,128,256]{4,3,2,1,0:T(8,128)(2,1)} %fusion.24), calls=%async_computation.2 | async-start | bytes 8388608 | tf_op jit(solution)/shard_map/all_to_all | solution.py:10
  262.9 6.0 %fusion.159 = (bf16[4,512,1024]{2,1,0:T(8,128)(2,1)}, bf16[4,512,1024]{2,1,0:T(8,128)(2,1)}) fusion(bf16[4,1024,1024]{2,1,0:T(8,128)(2,1)} %param.13), kind=kLoop, calls=%fused_computation.250 | loop fusion | bytes 16777216 | tf_op jit(solution)/shard_map/jit(_take)/gather | solution.py:100
  268.9 5.0 %gather_fusion = bf16[4,512,1024]{2,1,0:T(8,128)(2,1)} fusion(bf16[4,512,1024]{2,1,0:T(8,128)(2,1)} %get-tuple-element.7, s32[1024]{0:T(1024)S(1)} %pad_clamp_fusion), kind=kCustom, calls=%fused_computation | custom fusion | bytes 8388624 | tf_op jit(solution)/shard_map/jit(_take)/gather | solution.py:100
  273.8 5.0 %gather_fusion.1 = bf16[4,512,1024]{2,1,0:T(8,128)(2,1)} fusion(bf16[4,512,1024]{2,1,0:T(8,128)(2,1)} %get-tuple-element.8, s32[1024]{0:T(1024)S(1)} %pad_clamp_fusion), kind=kCustom, calls=%fused_computation.1 | custom fusion | bytes 8388624 | tf_op jit(solution)/shard_map/jit(_take)/gather | solution.py:100
  278.8 43.0 %all-to-all-done.2 = bf16[8,2,4,128,256]{4,3,2,1,0:T(8,128)(2,1)} async-done(((bf16[8,2,4,128,256]{4,3,2,1,0:T(8,128)(2,1)}), bf16[8,2,4,128,256]{4,3,2,1,0:T(8,128)(2,1)}, u32[]{:S(2)}, u32[]{:S(2)}) %all-to-all-start.2) | async-done | bytes 4194336 | tf_op jit(solution)/shard_map/all_to_all | solution.py:10
  321.8 7.5 %copy.32 = bf16[2,4,8,128,256]{3,2,4,0,1:T(8,128)(2,1)} copy(bf16[2,4,8,128,256]{4,3,1,0,2:T(8,128)(2,1)} %bitcast.34) | data formatting | bytes 8388608 | tf_op jit(solution)/shard_map/reshape | solution.py:9
  329.3 7.3 %reshape.210 = bf16[2,4,1024,256]{2,3,0,1:T(8,128)(2,1)} reshape(bf16[2,4,8,128,256]{3,2,4,0,1:T(8,128)(2,1)} %copy.32) | data formatting | bytes 8388608 | tf_op jit(solution)/shard_map/reshape | solution.py:9
  336.5 11.2 %convert_bitcast_fusion = bf16[2,4,1024,256]{2,3,0,1:T(8,128)(2,1)} fusion(bf16[2,4,1024,256]{2,3,0,1:T(8,128)(2,1)} %reshape.210, bf16[4,512,1024]{2,1,0:T(8,128)(2,1)} %gather_fusion.1, bf16[4,512,1024]{2,1,0:T(8,128)(2,1)} %gather_fusion, pred[4]{0:T(512)(128)(4,1)S(1)} %and_bitcast_fusion), kind=kOutput, calls=%fused_computation.19 | convolution fusion | flops 4318035968 | bytes 16777220 | tf_op jit(solution)/shard_map/bgf,cbfm->cbgm/dot_general | solution.py:102
  347.7 6.2 %copy.33 = bf16[2,4,1024,256]{3,2,1,0:T(8,128)(2,1)} copy(bf16[2,4,1024,256]{2,3,0,1:T(8,128)(2,1)} %convert_bitcast_fusion) | data formatting | bytes 8388608 | tf_op jit(solution)/shard_map/convert_element_type | solution.py:107
  (18 shorter events, 3.0 us)
Async XLA Ops:
  1.3 7.6 %collective-permute-start = (f32[128,16]{1,0:T(8,128)S(1)}, f32[128,16]{1,0:T(8,128)S(1)}, u32[]{:S(2)}, u32[]{:S(2)}) collective-permute-start(f32[128,16]{1,0:T(8,128)S(1)} %get-tuple-element.11), channel_id=1, source_target_pairs={{0,8},{8,16},{16,24},{24,32},{32,40},{40,48},{48,56},{56,64},{64,7... | collective-permute-start | bytes 24584 | tf_op jit(solution)/shard_map/ppermute | solution.py:27
  1.3 7.6 %collective-permute-start.1 = (f32[128,16]{1,0:T(8,128)S(1)}, f32[128,16]{1,0:T(8,128)S(1)}, u32[]{:S(2)}, u32[]{:S(2)}) collective-permute-start(f32[128,16]{1,0:T(8,128)S(1)} %get-tuple-element.12), channel_id=1, source_target_pairs={{8,0},{16,8},{24,16},{32,24},{40,32},{48,40},{56,48},{64,56},{72,6... | collective-permute-start | bytes 24584 | tf_op jit(solution)/shard_map/ppermute | solution.py:28
  17.7 59.3 %all-to-all-start = ((bf16[2,32,128,256]{3,1,0,2:T(8,128)(2,1)}), bf16[2,32,128,256]{3,1,0,2:T(8,128)(2,1)}, u32[]{:S(2)}, u32[]{:S(2)}) async-start(bf16[2,32,128,256]{3,1,0,2:T(8,128)(2,1)} %multiply_convert_fusion), calls=%async_computation | async-start | bytes 8388608 | tf_op jit(solution)/shard_map/all_to_all | solution.py:98
  246.0 7.7 %copy-start = (bf16[2,32,16,8,256]{4,3,2,1,0:T(8,128)(2,1)S(1)}, bf16[2,32,16,8,256]{4,3,2,1,0:T(8,128)(2,1)}, u32[]{:S(2)}) copy-start(bf16[2,32,16,8,256]{4,3,2,1,0:T(8,128)(2,1)} %copy.31) | copy-start | bytes 12582916
  257.1 5.7 %copy-start.1 = (s32[4,1]{0,1:T(1,128)S(1)}, s32[4,1]{0,1:T(1,128)}, u32[]{:S(2)}) copy-start(s32[4,1]{0,1:T(1,128)} %param.12) | copy-start | bytes 52
  257.1 64.7 %all-to-all-start.2 = ((bf16[8,2,4,128,256]{4,3,2,1,0:T(8,128)(2,1)}), bf16[8,2,4,128,256]{4,3,2,1,0:T(8,128)(2,1)}, u32[]{:S(2)}, u32[]{:S(2)}) async-start(bf16[8,2,4,128,256]{4,3,2,1,0:T(8,128)(2,1)} %fusion.24), calls=%async_computation.2 | async-start | bytes 8388608 | tf_op jit(solution)/shard_map/all_to_all | solution.py:10
